TPU v7x, 128 devices: a whole 4x4x4 slice. The times are simulated.
128 devices in a mesh: dp: 32 (over z, x_hi, y), own: 4 (over x_lo, core).
Axes of the slice: x: 4 (x_hi: 2, x_lo: 2; x = x_hi * 2 + x_lo), y: 4, z: 4, core: 2. Of those that a mesh axis runs over, the one named last changes fastest.
Arguments:
- tokens: bfloat16 [4096, 6144], P('dp', 'own'), may hold values from -6 to 6
- expert_ids: int32 [4096, 2], P('dp'), may hold values from 0 to 7, all different within a row; in each aligned block of 128 rows (0 to 127, 128 to 255, ...) at most 40 rows name the same one
- combine_weights: float32 [4096, 2], P('dp'), may hold values from 0.2 to 1
- gate_weight: bfloat16 [2, 6144, 8192], P(None, 'own', 'dp'), may hold values from -0.078125 to 0.078125
- up_weight: bfloat16 [2, 6144, 8192], P(None, 'own', 'dp'), may hold values from -0.078125 to 0.078125
- down_weight: bfloat16 [2, 8192, 6144], P(None, 'dp', 'own'), may hold values from -0.0625 to 0.0625
- out_grad: bfloat16 [4096, 6144], P('dp', 'own'), may hold values from -6 to 6
Outputs:
- mixed: bfloat16 [4096, 6144], P('dp', 'own')
- token_grad: bfloat16 [4096, 6144], P('dp', 'own')
- gate_grad_weight: float32 [2, 6144, 8192], P(None, 'own', 'dp')
- up_grad_weight: float32 [2, 6144, 8192], P(None, 'own', 'dp')
- down_grad_weight: float32 [2, 8192, 6144], P(None, 'dp', 'own')
Inputs may be any that keep to these rules, and one draw needn't show every extreme that they name: `expert_ids`: each row names 2 different experts. The 128 rows of one index of dp name each expert at most 40 times, and in every draw some expert is named exactly 40 times by the rows of one index of dp.
All inputs are finite; a program needn't handle non-finite values.
Results may differ from a plain program's by a relative error of at most 0.024.
Values may be sent and summed in bfloat16 or wider, within the bound.
A program may use at most 192 MiB of HBM per device.

v0:
```python
import jax
import jax.numpy as jnp
from jax import lax
from jax.experimental import pallas as pl
from jax.experimental.pallas import tpu as pltpu
from jax.sharding import PartitionSpec as P

CAP = 40
RING = 4
CHUNK = RING * CAP
HALF = CHUNK // 2
TILE = 256
MESH = pl.DeviceIdType.MESH
F32 = jnp.float32
BF16 = jnp.bfloat16
MESSAGES = ((0, 1, 0), (1, 1, 0), (0, -1, 0), (1, -1, 0), (0, 1, -1), (1, -1, 1))


def dp_of(z, x, y):
    return z * 8 + x * 4 + y


def place():
    dp, own = lax.axis_index("dp"), lax.axis_index("own")
    z, x, y = dp // 8, (dp // 4) % 2, dp % 4
    core, low = own % 2, own // 2

    def along(axis, step):
        if axis == "y":
            return (dp_of(z, x, (y + step + RING) % RING), own)
        return (dp_of((z + step + RING) % RING, x, y), own)

    partner = (dp_of(z, 1 - x, y), own)
    sibling = (dp, low * 2 + (1 - core))
    across = (dp, (1 - low) * 2 + core)
    return z, x, y, core, along, partner, sibling, across


def send(src, dst, send_sem, recv_sem, device):
    return pltpu.make_async_remote_copy(
        src_ref=src, dst_ref=dst, send_sem=send_sem, recv_sem=recv_sem, device_id=device, device_id_type=MESH
    )


def meet(devices):
    barrier = pltpu.get_barrier_semaphore()
    for device in devices:
        pl.semaphore_signal(barrier, inc=1, device_id=device, device_id_type=MESH)
    return barrier, len(devices)


def nt(a, b):
    return lax.dot_general(a, b, (((1,), (1,)), ((), ())), preferred_element_type=F32)


def nn(a, b):
    return jnp.dot(a, b, preferred_element_type=F32)


def tn(a, b):
    return lax.dot_general(a, b, (((0,), (0,)), ((), ())), preferred_element_type=F32)


def layer_kernel(
    tok, ids, mix, grad, wg_h, wu_h, wd_h,
    mixed, token_grad, dg_h, du_h, dd_h, x_all,
    mine, hot, wg, wu, wd, xin, part, r1, s1, r2, act,
    pb, rd, rb, s2, td, tb, ts, x3, rx3, win, wout,
    load_sem, put_sem, xin_sem, win_sem, wout_sem,
    ag_send, ag_recv, x_send, x_recv, own_send, own_recv, c_send, c_recv, y_send, y_recv,
):
    z, x, y, core, along, partner, sibling, across = place()
    first, second = ("y", "z"), ("z", "y")
    coord = {"y": y, "z": z}
    width = wd.shape[-1]
    tiles = width // TILE
    loads = [
        pltpu.make_async_copy(src, dst, load_sem.at[i])
        for i, (src, dst) in enumerate(((wg_h, wg), (wu_h, wu), (wd_h, wd)))
    ]
    for load in loads:
        load.start()
    barrier, count = meet(
        (along("y", 1), along("y", -1), along("z", 1), along("z", -1), partner, sibling, across)
    )
    shard = tok.shape[0]
    earlier = lax.broadcasted_iota(jnp.int32, (shard, shard), 1) < lax.broadcasted_iota(
        jnp.int32, (shard, shard), 0
    )
    slots = lax.broadcasted_iota(jnp.int32, (shard, CAP), 1).astype(F32)
    weight = []
    for e in range(2):
        chosen = (ids[...] == e).astype(F32)
        routed = jnp.sum(chosen, axis=1, keepdims=True)
        weight.append(jnp.sum(chosen * mix[...], axis=1, keepdims=True))
        spread = jnp.broadcast_to(routed, (shard, 128)).astype(BF16)
        position = nn(earlier.astype(F32).astype(BF16), spread)[:, 0:1]
        hot[e] = jnp.where((routed > 0.0) & (position == slots), 1.0, 0.0).astype(BF16)
        mine[0, e] = tn(hot[e], tok[...]).astype(BF16)
        mine[1, e] = tn(hot[e], (weight[e] * grad[...].astype(F32)).astype(BF16)).astype(BF16)
    pl.semaphore_wait(barrier, count)

    def plane(wave):
        return x if wave == 0 else 1 - x

    def q_of(e):
        return z + e * (y - z)

    def piece(t, e, xs, qc, pc):
        row = pl.multiple_of((xs * 16 + qc * 4 + pc) * CAP, 8)
        return x_all.at[t, e, pl.ds(row, CAP)]

    def chunk(t, e, xs, qc):
        row = pl.multiple_of((xs * 4 + qc) * CHUNK, 32)
        return x_all.at[t, e, pl.ds(row, CHUNK)]

    def phase(wave, e, stage, m, arriving=False):
        t, way, shift = MESSAGES[m]
        axis = (first if stage == 0 else second)[e]
        a, b, xs = coord[first[e]], coord[second[e]], plane(wave)
        if arriving:
            shift = shift - way
        if stage == 0:
            ref = piece(t, e, xs, b, (a + shift + RING) % RING)
            src = mine.at[t, e] if wave == 0 and m < 4 and not arriving else ref
        else:
            ref = chunk(t, e, xs, (b + shift + RING) % RING)
            src = ref
        index = ((wave * 2 + e) * 2 + stage) * 6 + m
        return send(src, ref, ag_send.at[index], ag_recv.at[index], along(axis, way))

    def start(wave, stage, messages):
        for m in messages:
            for e in range(2):
                phase(wave, e, stage, m).start()

    def arrive(wave, stage, messages):
        for m in messages:
            for e in range(2):
                phase(wave, e, stage, m, True).wait_recv()

    def relay(wave, stage):
        for came, out in ((0, 4), (3, 5)):
            arrive(wave, stage, (came,))
            start(wave, stage, (out,))

    puts, crossings, landings = [], [], []
    for t in range(2):
        for e in range(2):
            a, b, i = coord[first[e]], coord[second[e]], t * 2 + e
            puts.append(pltpu.make_async_copy(mine.at[t, e], piece(t, e, x, b, a), put_sem.at[i]))
            crossings.append(send(mine.at[t, e], piece(t, e, x, b, a), x_send.at[i], x_recv.at[i], partner))
            theirs = piece(t, e, 1 - x, b, a)
            landings.append(send(mine.at[t, e], theirs, x_send.at[i], x_recv.at[i], partner))

    steps = [(wave, shift) for wave in range(2) for shift in (0, -1, 1, 2)]

    def row_of(e, wave, shift):
        return (plane(wave) * 4 + (q_of(e) + shift + RING) % RING) * CHUNK

    def own_one(step, e):
        i = step * 2 + e
        far = pl.multiple_of((1 - core) * HALF, HALF)
        return send(part.at[i, :, pl.ds(far, HALF)], r1.at[i], own_send.at[i], own_recv.at[i], sibling)

    def own_two(step, e):
        i = step * 2 + e
        return send(s1.at[i], r2.at[i], own_send.at[16 + i], own_recv.at[16 + i], across)

    def own_three(step, e, arriving=False):
        i = step * 2 + e
        wave, shift = steps[step]
        side = 1 - core if arriving else core
        row = pl.multiple_of(row_of(e, wave, shift) + side * HALF, 16)
        ref = act.at[:, e, pl.ds(row, HALF)]
        return send(ref, ref, own_send.at[32 + i], own_recv.at[32 + i], sibling)

    def fetch(step):
        wave, shift = steps[step]
        return [
            pltpu.make_async_copy(
                chunk(t, e, plane(wave), (q_of(e) + shift + RING) % RING), xin.at[t, e], xin_sem.at[t * 2 + e]
            )
            for t in range(2)
            for e in range(2)
        ]

    def matmuls(step):
        def one(e, carry):
            i = step * 2 + e
            part[i, 0] = nn(xin[0, e], wg[e]).astype(BF16)
            part[i, 1] = nn(xin[0, e], wu[e]).astype(BF16)
            part[i, 2] = nt(xin[1, e], wd[e]).astype(BF16)
            own_one(step, e).start()
            return carry

        lax.fori_loop(0, 2, one, 0)

    def halves(step):
        def one(e, carry):
            i = step * 2 + e
            own_one(step, e).wait_recv()
            near = pl.multiple_of(core * HALF, HALF)
            for k in range(3):
                total = part[i, k, pl.ds(near, HALF), :].astype(F32) + r1[i, k].astype(F32)
                s1[i, k] = total.astype(BF16)
            own_two(step, e).start()
            return carry

        lax.fori_loop(0, 2, one, 0)

    def gates(step):
        wave, shift = steps[step]

        def one(e, carry):
            i = step * 2 + e
            own_two(step, e).wait_recv()
            row = pl.multiple_of(row_of(e, wave, shift) + core * HALF, 16)
            gate = s1[i, 0].astype(F32) + r2[i, 0].astype(F32)
            up = s1[i, 1].astype(F32) + r2[i, 1].astype(F32)
            back = s1[i, 2].astype(F32) + r2[i, 2].astype(F32)
            sigma = jax.nn.sigmoid(gate)
            swish = gate * sigma
            act[0, e, pl.ds(row, HALF), :] = (swish * up).astype(BF16)
            act[1, e, pl.ds(row, HALF), :] = (back * up * sigma * (1.0 + gate * (1.0 - sigma))).astype(BF16)
            act[2, e, pl.ds(row, HALF), :] = (back * swish).astype(BF16)
            own_three(step, e).start()
            return carry

        lax.fori_loop(0, 2, one, 0)

    def compute(step):
        copies = fetch(step)
        for copy in copies:
            copy.start()
        if step >= 2:
            gates(step - 2)
        for copy in copies:
            copy.wait()
        matmuls(step)
        if step >= 1:
            halves(step - 1)

    def settled(group):
        for step in group:
            for e in range(2):
                own_three(step, e, True).wait_recv()

    def hop(side, e, stage, m):
        t = m % 2
        way = (1, -1, 1, -1, -1, 1)[m]
        axis = (second if stage == 0 else first)[e]
        index = ((side * 2 + e) * 2 + stage) * 6 + m
        if stage == 0:
            src = pb.at[side, (3, 3, 1, 2, 2, 1)[m], t, e]
            dst = rd.at[side, t, e] if m < 2 else rb.at[side, (m - 2) // 2, t, e]
        else:
            a = coord[first[e]]
            far = s2.at[side, t, e, (a + 2) % RING]
            near = s2.at[side, t, e, (a + way + RING) % RING]
            src = far if m < 2 else ts.at[side, t, e] if m < 4 else near
            dst = td.at[side, t, e] if m < 2 else tb.at[side, (m - 2) // 2, t, e]
        return send(src, dst, c_send.at[index], c_recv.at[index], along(axis, way))

    def go(side, stage, messages):
        for m in messages:
            for e in range(2):
                hop(side, e, stage, m).start()

    def come(side, stage, messages):
        for m in messages:
            for e in range(2):
                hop(side, e, stage, m).wait_recv()

    def over_tiles(one):
        def step(i, carry):
            e, n = i // tiles, i % tiles
            one(e, pl.ds(pl.multiple_of(n * TILE, TILE), TILE))
            return carry

        lax.fori_loop(0, 2 * tiles, step, 0)

    def produce(side, j):
        shift = (0, 1, -1, 2)[j]

        def one(e, col):
            rows = pl.ds(pl.multiple_of(row_of(e, 1 - side, shift), 32), CHUNK)
            pb[side, j, 0, e, :, col] = nn(act[0, e, rows, :], wd[e, :, col]).astype(BF16)
            back = nt(act[1, e, rows, :], wg[e, col, :]) + nt(act[2, e, rows, :], wu[e, col, :])
            pb[side, j, 1, e, :, col] = back.astype(BF16)

        over_tiles(one)

    def relay_first(side):
        for t in range(2):
            come(side, 0, (t,))

            def one(e, col):
                total = pb[side, 1 + t, t, e, :, col].astype(F32) + rd[side, t, e, :, col].astype(F32)
                pb[side, 1 + t, t, e, :, col] = total.astype(BF16)

            over_tiles(one)
            go(side, 0, (2 + t,))

    def gather_first(side):
        come(side, 0, (2, 3, 4, 5))
        for t in range(2):

            def one(e, col):
                total = (
                    pb[side, 0, t, e, :, col].astype(F32)
                    + rb[side, 0, t, e, :, col].astype(F32)
                    + rb[side, 1, t, e, :, col].astype(F32)
                )
                for k in range(RING):
                    s2[side, t, e, k, :, col] = total[k * CAP : (k + 1) * CAP].astype(BF16)

            over_tiles(one)
        go(side, 1, (0, 1, 4, 5))

    def relay_second(side):
        for t in range(2):
            come(side, 1, (t,))
            for e in range(2):
                a = coord[first[e]]
                near = (a + (1, -1)[t] + RING) % RING
                total = s2[side, t, e, near].astype(F32) + td[side, t, e].astype(F32)
                ts[side, t, e] = total.astype(BF16)
            go(side, 1, (2 + t,))

    def total_second(side, t, e):
        a = coord[first[e]]
        return (
            s2[side, t, e, a].astype(F32)
            + tb[side, 0, t, e].astype(F32)
            + tb[side, 1, t, e].astype(F32)
        )

    def crossing(t, e):
        i = t * 2 + e
        return send(x3.at[t, e], rx3.at[t, e], y_send.at[i], y_recv.at[i], partner)

    def weight_in(i, slot):
        e, n = i // tiles, i % tiles
        col = pl.ds(pl.multiple_of(n * TILE, TILE), TILE)
        return [
            pltpu.make_async_copy(x_all.at[t, e, :, col], win.at[slot, t], win_sem.at[slot, t]) for t in range(2)
        ]

    def weight_out(i, slot):
        e, n = i // tiles, i % tiles
        col = pl.ds(pl.multiple_of(n * TILE, TILE), TILE)
        return [
            pltpu.make_async_copy(wout.at[slot, 0], dg_h.at[e, col], wout_sem.at[slot, 0]),
            pltpu.make_async_copy(wout.at[slot, 1], du_h.at[e, col], wout_sem.at[slot, 1]),
            pltpu.make_async_copy(wout.at[slot, 2], dd_h.at[e, :, col], wout_sem.at[slot, 2]),
        ]

    last = 2 * tiles

    def weight_grads(begin, end):
        def step(i, carry):
            slot = i % 2
            for copy in weight_in(i, slot):
                copy.wait()

            @pl.when(i + 1 < last)
            def _():
                for copy in weight_in(i + 1, 1 - slot):
                    copy.start()

            @pl.when(i >= 2)
            def _():
                for copy in weight_out(i - 2, slot):
                    copy.wait()

            e = i // tiles
            wout[slot, 0] = tn(win[slot, 0], act[1, e])
            wout[slot, 1] = tn(win[slot, 0], act[2, e])
            wout[slot, 2] = tn(act[0, e], win[slot, 1])
            for copy in weight_out(i, slot):
                copy.start()
            return carry

        lax.fori_loop(begin, end, step, 0)

    order = (0, 3, 1, 2)
    start(0, 0, order)
    for copy in crossings + puts:
        copy.start()
    relay(0, 0)
    arrive(0, 0, (1, 2, 4, 5))
    for copy in puts:
        copy.wait()
    start(0, 1, order)
    for copy in landings:
        copy.wait_recv()
    start(1, 0, order)
    for load in loads:
        load.wait()
    compute(0)
    relay(1, 0)
    relay(0, 1)
    arrive(1, 0, (1, 2, 4, 5))
    start(1, 1, order)
    arrive(0, 1, (1,))
    compute(1)
    arrive(0, 1, (2,))
    compute(2)
    arrive(0, 1, (4, 5))
    compute(3)
    compute(4)
    relay(1, 1)
    arrive(1, 1, (1,))
    compute(5)
    arrive(1, 1, (2,))
    compute(6)
    settled((0, 1, 2, 3))
    produce(1, 3)
    produce(1, 1)
    produce(1, 2)
    produce(1, 0)
    arrive(1, 1, (4, 5))
    go(1, 0, (0, 1, 5, 4))
    compute(7)
    gates(6)
    halves(7)
    for copy in weight_in(0, 0):
        copy.start()
    gates(7)
    settled((4, 5, 6, 7))
    produce(0, 3)
    go(0, 0, (0, 1))
    produce(0, 1)
    go(0, 0, (5,))
    produce(0, 2)
    go(0, 0, (4,))
    produce(0, 0)
    weight_grads(0, 4)
    relay_first(0)
    relay_first(1)
    weight_grads(4, 8)
    gather_first(0)
    weight_grads(8, 10)
    relay_second(0)
    weight_grads(10, last)
    come(0, 1, (2, 3, 4, 5))
    for t in range(2):
        for e in range(2):
            x3[t, e] = total_second(0, t, e).astype(BF16)
            crossing(t, e).start()
    gather_first(1)
    relay_second(1)
    come(1, 1, (2, 3, 4, 5))
    final = [[None, None], [None, None]]
    for t in range(2):
        for e in range(2):
            crossing(t, e).wait_recv()
            final[t][e] = (total_second(1, t, e) + rx3[t, e].astype(F32)).astype(BF16)
    mixed[...] = (weight[0] * nn(hot[0], final[0][0]) + weight[1] * nn(hot[1], final[0][1])).astype(BF16)
    token_grad[...] = (nn(hot[0], final[1][0]) + nn(hot[1], final[1][1])).astype(BF16)
    for i in (last - 2, last - 1):
        for copy in weight_out(i, i % 2):
            copy.wait()
    for e in range(2):
        for wave in range(2):
            for stage in range(2):
                for m in range(6):
                    phase(wave, e, stage, m).wait_send()
                    hop(wave, e, stage, m).wait_send()
        for t in range(2):
            crossings[t * 2 + e].wait_send()
            crossing(t, e).wait_send()
        for step in range(8):
            own_one(step, e).wait_send()
            own_two(step, e).wait_send()
            own_three(step, e).wait_send()


def local(tokens, expert_ids, combine_weights, gate_weight, up_weight, down_weight, out_grad):
    shard, width = tokens.shape
    experts, hidden = gate_weight.shape[0], gate_weight.shape[2]
    rows = 32 * CAP
    vmem = pl.BlockSpec(memory_space=pltpu.VMEM)
    hbm = pl.BlockSpec(memory_space=pl.ANY)
    dma = pltpu.SemaphoreType.DMA
    out = jax.ShapeDtypeStruct((shard, width), BF16)
    result = pl.pallas_call(
        layer_kernel,
        out_shape=(
            out,
            out,
            jax.ShapeDtypeStruct(gate_weight.shape, F32),
            jax.ShapeDtypeStruct(up_weight.shape, F32),
            jax.ShapeDtypeStruct(down_weight.shape, F32),
            jax.ShapeDtypeStruct((2, experts, rows, width), BF16),
        ),
        in_specs=[vmem] * 4 + [hbm] * 3,
        out_specs=(vmem,) * 2 + (hbm,) * 4,
        scratch_shapes=[
            pltpu.VMEM((2, 2, CAP, width), BF16),
            pltpu.VMEM((2, shard, CAP), BF16),
            pltpu.VMEM(gate_weight.shape, BF16),
            pltpu.VMEM(up_weight.shape, BF16),
            pltpu.VMEM(down_weight.shape, BF16),
            pltpu.VMEM((2, 2, CHUNK, width), BF16),
            pltpu.VMEM((16, 3, CHUNK, hidden), BF16),
            pltpu.VMEM((16, 3, HALF, hidden), BF16),
            pltpu.VMEM((16, 3, HALF, hidden), BF16),
            pltpu.VMEM((16, 3, HALF, hidden), BF16),
            pltpu.VMEM((3, 2, rows, hidden), BF16),
            pltpu.VMEM((2, 4, 2, 2, CHUNK, width), BF16),
            pltpu.VMEM((2, 2, 2, CHUNK, width), BF16),
            pltpu.VMEM((2, 2, 2, 2, CHUNK, width), BF16),
            pltpu.VMEM((2, 2, 2, RING, CAP, width), BF16),
            pltpu.VMEM((2, 2, 2, CAP, width), BF16),
            pltpu.VMEM((2, 2, 2, 2, CAP, width), BF16),
            pltpu.VMEM((2, 2, 2, CAP, width), BF16),
            pltpu.VMEM((2, 2, CAP, width), BF16),
            pltpu.VMEM((2, 2, CAP, width), BF16),
            pltpu.VMEM((2, 2, rows, TILE), BF16),
            pltpu.VMEM((2, 3, TILE, TILE), F32),
            dma((3,)),
            dma((4,)),
            dma((4,)),
            dma((2, 2)),
            dma((2, 3)),
            dma((48,)),
            dma((48,)),
            dma((4,)),
            dma((4,)),
            dma((48,)),
            dma((48,)),
            dma((48,)),
            dma((48,)),
            dma((4,)),
            dma((4,)),
        ],
        compiler_params=pltpu.CompilerParams(
            collective_id=0, has_side_effects=True, vmem_limit_bytes=67000000
        ),
        name="layer",
    )(tokens, expert_ids, combine_weights, out_grad, gate_weight, up_weight, down_weight)
    return result[:5]


def solution(mesh):
    in_specs = (
        P("dp", "own"),
        P("dp", None),
        P("dp", None),
        P(None, "own", "dp"),
        P(None, "own", "dp"),
        P(None, "dp", "own"),
        P("dp", "own"),
    )
    out_specs = (
        P("dp", "own"),
        P("dp", "own"),
        P(None, "own", "dp"),
        P(None, "own", "dp"),
        P(None, "dp", "own"),
    )
    return jax.shard_map(local, mesh=mesh, in_specs=in_specs, out_specs=out_specs, check_vma=False)
```

profile of v0, /device:TPU:1, one launch (start us, length us, event | category | flops | bytes accessed | tf_op | source)
XLA Modules:
  0.0 220.3 jit_solution(16451417001577046446)
XLA Ops:
  0.6 1.4 copy.12.ids
  2.0 1.4 copy.13.mix
  3.5 204.6 %layer.1 = (bf16[128,1536]{1,0:T(8,128)(2,1)}, bf16[128,1536]{1,0:T(8,128)(2,1)}, f32[2,1536,256]{2,1,0:T(8,128)}, f32[2,1536,256]{2,1,0:T(8,128)}, f32[2,256,15...) custom-call(bf16[128,1536]{1,0:T(8,128)(2,1)} %tok.1, s32[128,2]{1,0:T(8,128)} %copy.12.ids, f32[128,2]{1,0:T(8,128)} %copy.13.mix, ...), custom_call_target="tpu_custom_call" | custom-call | tf_op jit(solution)/shard_map/layer/pallas_call | solution.py:488
  208.1 1.8 copy.19
  209.9 1.8 copy.20
  211.6 0.0 copy-start.1
  211.6 3.9 %copy.21 = f32[2,1536,256]{2,1,0:T(8,128)} copy(f32[2,1536,256]{2,1,0:T(8,128)} %get-tuple-element.22) | data formatting | bytes 6291456
  215.6 0.0 copy-done.1
  215.6 0.0 copy-start
  215.6 1.7 copy.22
  217.2 1.4 copy-done
  218.6 1.7 copy.23
Async XLA Ops:
  211.6 3.9 %copy-start.1 = (f32[2,1536,256]{2,1,0:T(8,128)S(1)}, f32[2,1536,256]{2,1,0:T(8,128)}, u32[]{:S(2)}) copy-start(f32[2,1536,256]{2,1,0:T(8,128)} %get-tuple-element.23) | copy-start | bytes 9437188
  215.6 3.0 %copy-start = (f32[2,256,1536]{2,1,0:T(8,128)S(1)}, f32[2,256,1536]{2,1,0:T(8,128)}, u32[]{:S(2)}) copy-start(f32[2,256,1536]{2,1,0:T(8,128)} %get-tuple-element.24) | copy-start | bytes 9437188
where the time goes:
time: 221 us; the launch traced here: 220 us
  Pallas kernels  205 us (93%)
  local copies, waits for them, and re-layouts  15 us (7%)
    pallas_call x1, Pallas kernels, local(): pl.pallas_call(layer_kernel, out_shape=(out, out, jax.ShapeDtypeStruct(ga...  205 us
    unnamed x11, local copies, waits for them, and re-layouts  15 us

commit v1 on v0

--- a/solution.py
+++ b/solution.py
@@ -10,6 +10,7 @@
 CHUNK = RING * CAP
 HALF = CHUNK // 2
 TILE = 256
+SHARE = 80
 MESH = pl.DeviceIdType.MESH
 F32 = jnp.float32
 BF16 = jnp.bfloat16
@@ -67,7 +68,7 @@
     mine, hot, wg, wu, wd, xin, part, r1, s1, r2, act,
     pb, rd, rb, s2, td, tb, ts, x3, rx3, win, wout,
     load_sem, put_sem, xin_sem, win_sem, wout_sem,
-    ag_send, ag_recv, x_send, x_recv, own_send, own_recv, c_send, c_recv, y_send, y_recv,
+    ag_send, ag_recv, sh_send, sh_recv, x_send, x_recv, own_send, own_recv, c_send, c_recv, y_send, y_recv,
 ):
     z, x, y, core, along, partner, sibling, across = place()
     first, second = ("y", "z"), ("z", "y")
@@ -110,24 +111,34 @@
         row = pl.multiple_of((xs * 16 + qc * 4 + pc) * CAP, 8)
         return x_all.at[t, e, pl.ds(row, CAP)]
 
-    def chunk(t, e, xs, qc):
-        row = pl.multiple_of((xs * 4 + qc) * CHUNK, 32)
-        return x_all.at[t, e, pl.ds(row, CHUNK)]
+    def chunk(t, e, xs, qc, begin=0, end=CHUNK):
+        row = pl.multiple_of((xs * 4 + qc) * CHUNK + begin, 16)
+        return x_all.at[t, e, pl.ds(row, end - begin)]
 
     def phase(wave, e, stage, m, arriving=False):
         t, way, shift = MESSAGES[m]
         axis = (first if stage == 0 else second)[e]
         a, b, xs = coord[first[e]], coord[second[e]], plane(wave)
+        begin = 0
+        if wave == 1 and stage == 1:
+            t = 1 - t
+            begin = SHARE if m in (1, 2) else 0
         if arriving:
             shift = shift - way
         if stage == 0:
             ref = piece(t, e, xs, b, (a + shift + RING) % RING)
             src = mine.at[t, e] if wave == 0 and m < 4 and not arriving else ref
         else:
-            ref = chunk(t, e, xs, (b + shift + RING) % RING)
+            ref = chunk(t, e, xs, (b + shift + RING) % RING, begin)
             src = ref
         index = ((wave * 2 + e) * 2 + stage) * 6 + m
         return send(src, ref, ag_send.at[index], ag_recv.at[index], along(axis, way))
+
+    def share(t, e, arriving=False):
+        near = (coord[second[e]] + (-1, 1)[t] + RING) % RING
+        ref = chunk(t, e, 1 - x if arriving else x, near, 0, SHARE)
+        i = t * 2 + e
+        return send(ref, ref, sh_send.at[i], sh_recv.at[i], partner)
 
     def start(wave, stage, messages):
         for m in messages:
@@ -392,29 +403,36 @@
     arrive(0, 0, (1, 2, 4, 5))
     for copy in puts:
         copy.wait()
-    start(0, 1, order)
+    start(0, 1, (0, 3))
     for copy in landings:
         copy.wait_recv()
     start(1, 0, order)
+    start(0, 1, (1, 2))
     for load in loads:
         load.wait()
     compute(0)
+    arrive(0, 1, (0, 3))
+    for t in range(2):
+        for e in range(2):
+            share(t, e).start()
     relay(1, 0)
-    relay(0, 1)
-    arrive(1, 0, (1, 2, 4, 5))
-    start(1, 1, order)
+    start(0, 1, (4, 5))
     arrive(0, 1, (1,))
     compute(1)
+    arrive(1, 0, (1, 2, 4, 5))
+    start(1, 1, order if SHARE < CHUNK else (0, 3))
     arrive(0, 1, (2,))
     compute(2)
     arrive(0, 1, (4, 5))
     compute(3)
     compute(4)
     relay(1, 1)
-    arrive(1, 1, (1,))
-    compute(5)
-    arrive(1, 1, (2,))
-    compute(6)
+    for t, m in ((0, 1), (1, 2)):
+        if SHARE < CHUNK:
+            arrive(1, 1, (m,))
+        for e in range(2):
+            share(t, e, True).wait_recv()
+        compute(5 + t)
     settled((0, 1, 2, 3))
     produce(1, 3)
     produce(1, 1)
@@ -441,15 +459,14 @@
     relay_first(1)
     weight_grads(4, 8)
     gather_first(0)
-    weight_grads(8, 10)
+    weight_grads(8, last)
+    gather_first(1)
     relay_second(0)
-    weight_grads(10, last)
     come(0, 1, (2, 3, 4, 5))
     for t in range(2):
         for e in range(2):
             x3[t, e] = total_second(0, t, e).astype(BF16)
             crossing(t, e).start()
-    gather_first(1)
     relay_second(1)
     come(1, 1, (2, 3, 4, 5))
     final = [[None, None], [None, None]]
@@ -466,10 +483,12 @@
         for wave in range(2):
             for stage in range(2):
                 for m in range(6):
-                    phase(wave, e, stage, m).wait_send()
+                    if SHARE < CHUNK or (wave, stage) != (1, 1) or m not in (1, 2):
+                        phase(wave, e, stage, m).wait_send()
                     hop(wave, e, stage, m).wait_send()
         for t in range(2):
             crossings[t * 2 + e].wait_send()
+            share(t, e).wait_send()
             crossing(t, e).wait_send()
         for step in range(8):
             own_one(step, e).wait_send()
@@ -529,6 +548,8 @@
             dma((48,)),
             dma((4,)),
             dma((4,)),
+            dma((4,)),
+            dma((4,)),
             dma((48,)),
             dma((48,)),
             dma((48,)),

time: 221 us -> 217 us (0.982); the launches traced: 220 us -> 213 us
  Pallas kernels: 205 us -> 198 us
    pallas_call x1, Pallas kernels: 205 us -> 198 us  [local(): pl.pallas_call(layer_kernel, out_shape=(out, out, jax.ShapeDtypeStruct(ga...]
where the time goes in v1:
time: 217 us; the launch traced here: 213 us
  Pallas kernels  198 us (91%)
  local copies, waits for them, and re-layouts  15 us (7%)
    pallas_call x1, Pallas kernels, local(): pl.pallas_call(layer_kernel, out_shape=(out, out, jax.ShapeDtypeStruct(ga...  198 us
    unnamed x11, local copies, waits for them, and re-layouts  15 us

profile of v1, /device:TPU:1, one launch (start us, length us, event | category | flops | bytes accessed | tf_op | source)
XLA Modules:
  0.0 213.5 jit_solution(16482966695080006615)
XLA Ops:
  0.6 1.4 copy.12.ids
  2.0 1.4 copy.13.mix
  3.5 197.9 %layer.1 = (bf16[128,1536]{1,0:T(8,128)(2,1)}, bf16[128,1536]{1,0:T(8,128)(2,1)}, f32[2,1536,256]{2,1,0:T(8,128)}, f32[2,1536,256]{2,1,0:T(8,128)}, f32[2,256,15...) custom-call(bf16[128,1536]{1,0:T(8,128)(2,1)} %tok.1, s32[128,2]{1,0:T(8,128)} %copy.12.ids, f32[128,2]{1,0:T(8,128)} %copy.13.mix, ...), custom_call_target="tpu_custom_call" | custom-call | tf_op jit(solution)/shard_map/layer/pallas_call | solution.py:507
  201.4 1.8 copy.19
  203.1 1.8 copy.20
  204.9 0.0 copy-start.1
  204.9 3.9 %copy.21 = f32[2,1536,256]{2,1,0:T(8,128)} copy(f32[2,1536,256]{2,1,0:T(8,128)} %get-tuple-element.22) | data formatting | bytes 6291456
  208.8 0.0 copy-done.1
  208.8 0.0 copy-start
  208.8 1.7 copy.22
  210.5 1.4 copy-done
  211.8 1.7 copy.23
Async XLA Ops:
  204.9 3.9 %copy-start.1 = (f32[2,1536,256]{2,1,0:T(8,128)S(1)}, f32[2,1536,256]{2,1,0:T(8,128)}, u32[]{:S(2)}) copy-start(f32[2,1536,256]{2,1,0:T(8,128)} %get-tuple-element.23) | copy-start | bytes 9437188
  208.8 3.0 %copy-start = (f32[2,256,1536]{2,1,0:T(8,128)S(1)}, f32[2,256,1536]{2,1,0:T(8,128)}, u32[]{:S(2)}) copy-start(f32[2,256,1536]{2,1,0:T(8,128)} %get-tuple-element.24) | copy-start | bytes 9437188

commit v2 on v1

--- a/solution.py
+++ b/solution.py
@@ -435,11 +435,13 @@
         compute(5 + t)
     settled((0, 1, 2, 3))
     produce(1, 3)
+    go(1, 0, (0, 1))
     produce(1, 1)
+    go(1, 0, (5,))
     produce(1, 2)
+    go(1, 0, (4,))
     produce(1, 0)
     arrive(1, 1, (4, 5))
-    go(1, 0, (0, 1, 5, 4))
     compute(7)
     gates(6)
     halves(7)

time: 217 us -> 217 us (level)
  no operation moved by 1% of the time
where the time goes in v2:
time: 217 us; the launch traced here: 213 us
  Pallas kernels  198 us (91%)
  local copies, waits for them, and re-layouts  15 us (7%)
    pallas_call x1, Pallas kernels, local(): pl.pallas_call(layer_kernel, out_shape=(out, out, jax.ShapeDtypeStruct(ga...  198 us
    unnamed x11, local copies, waits for them, and re-layouts  15 us

profile of v2, /device:TPU:1, one launch (start us, length us, event | category | flops | bytes accessed | tf_op | source)
XLA Modules:
  0.0 213.5 jit_solution(4802930694138066869)
XLA Ops:
  0.6 1.4 copy.12.ids
  2.0 1.4 copy.13.mix
  3.5 197.9 %layer.1 = (bf16[128,1536]{1,0:T(8,128)(2,1)}, bf16[128,1536]{1,0:T(8,128)(2,1)}, f32[2,1536,256]{2,1,0:T(8,128)}, f32[2,1536,256]{2,1,0:T(8,128)}, f32[2,256,15...) custom-call(bf16[128,1536]{1,0:T(8,128)(2,1)} %tok.1, s32[128,2]{1,0:T(8,128)} %copy.12.ids, f32[128,2]{1,0:T(8,128)} %copy.13.mix, ...), custom_call_target="tpu_custom_call" | custom-call | tf_op jit(solution)/shard_map/layer/pallas_call | solution.py:509
  201.3 1.8 copy.19
  203.1 1.8 copy.20
  204.9 0.0 copy-start.1
  204.9 3.9 %copy.21 = f32[2,1536,256]{2,1,0:T(8,128)} copy(f32[2,1536,256]{2,1,0:T(8,128)} %get-tuple-element.22) | data formatting | bytes 6291456
  208.8 0.0 copy-done.1
  208.8 0.0 copy-start
  208.8 1.7 copy.22
  210.5 1.4 copy-done
  211.8 1.7 copy.23
Async XLA Ops:
  204.9 3.9 %copy-start.1 = (f32[2,1536,256]{2,1,0:T(8,128)S(1)}, f32[2,1536,256]{2,1,0:T(8,128)}, u32[]{:S(2)}) copy-start(f32[2,1536,256]{2,1,0:T(8,128)} %get-tuple-element.23) | copy-start | bytes 9437188
  208.8 3.0 %copy-start = (f32[2,256,1536]{2,1,0:T(8,128)S(1)}, f32[2,256,1536]{2,1,0:T(8,128)}, u32[]{:S(2)}) copy-start(f32[2,256,1536]{2,1,0:T(8,128)} %get-tuple-element.24) | copy-start | bytes 9437188
